TPU v7x, 512 devices: a whole 4x8x8 slice. The times are simulated.
512 devices in a mesh: head: 16 (over y, z_hi), seq: 32 (over x, z_lo, core).
Axes of the slice: x: 4, y: 8, z: 8 (z_hi: 2, z_lo: 4; z = z_hi * 4 + z_lo), core: 2. Of those that a mesh axis runs over, the one named last changes fastest.
Arguments:
- queries: bfloat16 [1, 32768, 8192], P(None, 'seq', 'head'), may hold values from -6 to 6
- keys: bfloat16 [1, 32768, 8192], P(None, 'seq', 'head'), may hold values from -6 to 6
- values: bfloat16 [1, 32768, 8192], P(None, 'seq', 'head'), may hold values from -60 to 60
- decay_rate: float32 [64], P('head'), may hold values from 1.5258789e-07 to 0.03
- norm_gain: float32 [8192], P('head'), may hold values from 0.25 to 1.75
- offsets: int32 [1], replicated, may hold values from 0 to 31
Outputs:
- normed: bfloat16 [1, 32768, 8192], P(None, 'seq', 'head')
All inputs are finite; a program needn't handle non-finite values.
Results may differ from a plain program's by a relative error of at most 0.0044.
Values sent between devices are 32-bit elements; how exact they have to be, the bound alone decides.
No kernel may reach another device: no remote copies, remote signals or barrier semaphores. Data moves between devices by JAX's collectives and lax.ppermute only.
A program may use at most 64 MiB of HBM per device.

v0:
```python
import jax
import jax.numpy as jnp
from jax import lax
from jax.sharding import PartitionSpec as P

epsilon = 1e-05


def from_behind(shard, axis, by):
    count = lax.axis_size(axis)
    return lax.ppermute(shard, axis, [(i, (i + by) % count) for i in range(count)])


def body(queries, keys, values, decay_rate, norm_gain, offsets):
    seq_count, block_len, columns = queries.shape
    heads_dev = decay_rate.shape[0]
    head_size = columns // heads_dev
    shaped = (seq_count, block_len, heads_dev, head_size)
    query_heads = queries.reshape(shaped)
    key_heads = keys.reshape(shaped)
    value_heads = values.reshape(shaped)
    places = jnp.arange(block_len).astype(jnp.float32)
    distance = places[:, None] - places[None, :]
    within = (
        jnp.exp(-decay_rate[:, None, None] * jnp.maximum(distance, 0.0)[None])
        * (distance >= 0.0).astype(jnp.float32)[None]
    )
    scores = jnp.einsum(
        "sihd,sjhd->shij", query_heads, key_heads, preferred_element_type=jnp.float32
    )
    weights = (scores * within[None]).astype(jnp.bfloat16)
    inner_part = jnp.einsum(
        "shij,sjhd->sihd", weights, value_heads, preferred_element_type=jnp.float32
    )
    key_scale = jnp.exp(-decay_rate[None, :] * (block_len - 1.0 - places[:, None]))
    decayed_keys = (key_heads.astype(jnp.float32) * key_scale[None, :, :, None]).astype(
        jnp.bfloat16
    )
    local_state = jnp.einsum(
        "sjhd,sjhe->shde", decayed_keys, value_heads, preferred_element_type=jnp.float32
    )
    group_decay = jnp.exp(-decay_rate * block_len)[None, :, None, None]
    cycle_size = lax.axis_size("seq")
    loop_place = lax.axis_index("seq")
    group_index = jnp.mod(loop_place - offsets, cycle_size)

    def follows(stride):
        return (group_index >= stride).astype(jnp.float32)[:, None, None, None]

    def advance(turn_index, incoming):
        outgoing = local_state + group_decay * incoming
        return follows(1) * from_behind(outgoing, "seq", 1)

    incoming = lax.fori_loop(0, cycle_size - 1, advance, jnp.zeros_like(local_state))
    query_scale = jnp.exp(-decay_rate[None, :] * (places[:, None] + 1.0))
    scaled_queries = query_heads.astype(jnp.float32) * query_scale[None, :, :, None]
    carried_part = jnp.einsum(
        "sihd,shde->sihe", scaled_queries, incoming, precision=lax.Precision.HIGHEST
    )
    attended = (inner_part + carried_part).reshape(seq_count, block_len, columns)
    squares = jnp.sum(attended * attended, axis=-1)
    sum_squares = lax.psum(squares, "head")
    features_all = columns * lax.axis_size("head")
    inv_rms = lax.rsqrt(sum_squares / features_all + epsilon)
    return (attended * inv_rms[..., None] * norm_gain).astype(jnp.bfloat16)


def solution(mesh):
    in_specs = (
        P(None, "seq", "head"),
        P(None, "seq", "head"),
        P(None, "seq", "head"),
        P("head"),
        P("head"),
        P(),
    )
    out_specs = P(None, "seq", "head")
    return jax.shard_map(body, mesh=mesh, in_specs=in_specs, out_specs=out_specs, check_vma=False)
```

profile of v0, /device:TPU:8, one launch (start us, length us, event | category | flops | bytes accessed | tf_op | source)
XLA Modules:
  0.0 450.2 jit_solution(8367281808237662304)
XLA Ops:
  7.3 365.9 %while.13 = (s32[]{:T(128)}, f32[1,4,128,128]{3,2,1,0:T(8,128)S(1)}, pred[1]{0:T(512)(128)(4,1)}, f32[1,4,1,1]{1,3,2,0:T(1,128)S(1)}, f32[1,4,128,128]{3,2,1,0:T(8,128)S(1)}, /*index=5*/s32[]{:T(128)}, s32[]{:T(128)}) while((s32[]{:T(128)}, f32[1,4,128,128]{3,2,1,0:T(8,128)S(1)}, pred[1]{0:T(512)(128)(4,1)}, ...), condition=%wide.region_1.2_spmd.clone, body=%wide.region_0.1_spmd.clone.sunk | while | flops 262148 | bytes 2359448 | solution.py:54
  7.4 1.9 collective-permute-start
  9.3 11.6 %collective-permute-done = f32[1,4,128,128]{3,2,1,0:T(8,128)S(1)} collective-permute-done((f32[1,4,128,128]{3,2,1,0:T(8,128)S(1)}, f32[1,4,128,128]{3,2,1,0:T(8,128)S(1)}, u32[]{:S(2)}, u32[]{:S(2)}) %collective-permute-start) | collective-permute-done | bytes 262176 | tf_op jit(solution)/shard_map/while/body/eval_jaxpr/ppermute | solution.py:11
  21.1 1.9 collective-permute-start
  23.0 9.7 %collective-permute-done = f32[1,4,128,128]{3,2,1,0:T(8,128)S(1)} collective-permute-done((f32[1,4,128,128]{3,2,1,0:T(8,128)S(1)}, f32[1,4,128,128]{3,2,1,0:T(8,128)S(1)}, u32[]{:S(2)}, u32[]{:S(2)}) %collective-permute-start) | collective-permute-done | bytes 262176 | tf_op jit(solution)/shard_map/while/body/eval_jaxpr/ppermute | solution.py:11
  32.8 1.9 collective-permute-start
  34.8 9.7 %collective-permute-done = f32[1,4,128,128]{3,2,1,0:T(8,128)S(1)} collective-permute-done((f32[1,4,128,128]{3,2,1,0:T(8,128)S(1)}, f32[1,4,128,128]{3,2,1,0:T(8,128)S(1)}, u32[]{:S(2)}, u32[]{:S(2)}) %collective-permute-start) | collective-permute-done | bytes 262176 | tf_op jit(solution)/shard_map/while/body/eval_jaxpr/ppermute | solution.py:11
  44.6 1.9 collective-permute-start
  46.5 9.7 %collective-permute-done = f32[1,4,128,128]{3,2,1,0:T(8,128)S(1)} collective-permute-done((f32[1,4,128,128]{3,2,1,0:T(8,128)S(1)}, f32[1,4,128,128]{3,2,1,0:T(8,128)S(1)}, u32[]{:S(2)}, u32[]{:S(2)}) %collective-permute-start) | collective-permute-done | bytes 262176 | tf_op jit(solution)/shard_map/while/body/eval_jaxpr/ppermute | solution.py:11
  56.3 1.9 collective-permute-start
  58.2 9.7 %collective-permute-done = f32[1,4,128,128]{3,2,1,0:T(8,128)S(1)} collective-permute-done((f32[1,4,128,128]{3,2,1,0:T(8,128)S(1)}, f32[1,4,128,128]{3,2,1,0:T(8,128)S(1)}, u32[]{:S(2)}, u32[]{:S(2)}) %collective-permute-start) | collective-permute-done | bytes 262176 | tf_op jit(solution)/shard_map/while/body/eval_jaxpr/ppermute | solution.py:11
  68.0 1.9 collective-permute-start
  70.0 9.7 %collective-permute-done = f32[1,4,128,128]{3,2,1,0:T(8,128)S(1)} collective-permute-done((f32[1,4,128,128]{3,2,1,0:T(8,128)S(1)}, f32[1,4,128,128]{3,2,1,0:T(8,128)S(1)}, u32[]{:S(2)}, u32[]{:S(2)}) %collective-permute-start) | collective-permute-done | bytes 262176 | tf_op jit(solution)/shard_map/while/body/eval_jaxpr/ppermute | solution.py:11
  79.8 1.9 collective-permute-start
  81.7 9.7 %collective-permute-done = f32[1,4,128,128]{3,2,1,0:T(8,128)S(1)} collective-permute-done((f32[1,4,128,128]{3,2,1,0:T(8,128)S(1)}, f32[1,4,128,128]{3,2,1,0:T(8,128)S(1)}, u32[]{:S(2)}, u32[]{:S(2)}) %collective-permute-start) | collective-permute-done | bytes 262176 | tf_op jit(solution)/shard_map/while/body/eval_jaxpr/ppermute | solution.py:11
  91.5 1.9 collective-permute-start
  93.4 9.7 %collective-permute-done = f32[1,4,128,128]{3,2,1,0:T(8,128)S(1)} collective-permute-done((f32[1,4,128,128]{3,2,1,0:T(8,128)S(1)}, f32[1,4,128,128]{3,2,1,0:T(8,128)S(1)}, u32[]{:S(2)}, u32[]{:S(2)}) %collective-permute-start) | collective-permute-done | bytes 262176 | tf_op jit(solution)/shard_map/while/body/eval_jaxpr/ppermute | solution.py:11
  103.2 1.9 collective-permute-start
  105.2 9.7 %collective-permute-done = f32[1,4,128,128]{3,2,1,0:T(8,128)S(1)} collective-permute-done((f32[1,4,128,128]{3,2,1,0:T(8,128)S(1)}, f32[1,4,128,128]{3,2,1,0:T(8,128)S(1)}, u32[]{:S(2)}, u32[]{:S(2)}) %collective-permute-start) | collective-permute-done | bytes 262176 | tf_op jit(solution)/shard_map/while/body/eval_jaxpr/ppermute | solution.py:11
  115.0 1.9 collective-permute-start
  116.9 9.7 %collective-permute-done = f32[1,4,128,128]{3,2,1,0:T(8,128)S(1)} collective-permute-done((f32[1,4,128,128]{3,2,1,0:T(8,128)S(1)}, f32[1,4,128,128]{3,2,1,0:T(8,128)S(1)}, u32[]{:S(2)}, u32[]{:S(2)}) %collective-permute-start) | collective-permute-done | bytes 262176 | tf_op jit(solution)/shard_map/while/body/eval_jaxpr/ppermute | solution.py:11
  126.7 1.9 collective-permute-start
  128.6 9.7 %collective-permute-done = f32[1,4,128,128]{3,2,1,0:T(8,128)S(1)} collective-permute-done((f32[1,4,128,128]{3,2,1,0:T(8,128)S(1)}, f32[1,4,128,128]{3,2,1,0:T(8,128)S(1)}, u32[]{:S(2)}, u32[]{:S(2)}) %collective-permute-start) | collective-permute-done | bytes 262176 | tf_op jit(solution)/shard_map/while/body/eval_jaxpr/ppermute | solution.py:11
  138.4 1.9 collective-permute-start
  140.4 9.7 %collective-permute-done = f32[1,4,128,128]{3,2,1,0:T(8,128)S(1)} collective-permute-done((f32[1,4,128,128]{3,2,1,0:T(8,128)S(1)}, f32[1,4,128,128]{3,2,1,0:T(8,128)S(1)}, u32[]{:S(2)}, u32[]{:S(2)}) %collective-permute-start) | collective-permute-done | bytes 262176 | tf_op jit(solution)/shard_map/while/body/eval_jaxpr/ppermute | solution.py:11
  150.2 1.9 collective-permute-start
  152.1 9.7 %collective-permute-done = f32[1,4,128,128]{3,2,1,0:T(8,128)S(1)} collective-permute-done((f32[1,4,128,128]{3,2,1,0:T(8,128)S(1)}, f32[1,4,128,128]{3,2,1,0:T(8,128)S(1)}, u32[]{:S(2)}, u32[]{:S(2)}) %collective-permute-start) | collective-permute-done | bytes 262176 | tf_op jit(solution)/shard_map/while/body/eval_jaxpr/ppermute | solution.py:11
  161.9 1.9 collective-permute-start
  163.9 9.7 %collective-permute-done = f32[1,4,128,128]{3,2,1,0:T(8,128)S(1)} collective-permute-done((f32[1,4,128,128]{3,2,1,0:T(8,128)S(1)}, f32[1,4,128,128]{3,2,1,0:T(8,128)S(1)}, u32[]{:S(2)}, u32[]{:S(2)}) %collective-permute-start) | collective-permute-done | bytes 262176 | tf_op jit(solution)/shard_map/while/body/eval_jaxpr/ppermute | solution.py:11
  173.7 1.9 collective-permute-start
  175.6 9.7 %collective-permute-done = f32[1,4,128,128]{3,2,1,0:T(8,128)S(1)} collective-permute-done((f32[1,4,128,128]{3,2,1,0:T(8,128)S(1)}, f32[1,4,128,128]{3,2,1,0:T(8,128)S(1)}, u32[]{:S(2)}, u32[]{:S(2)}) %collective-permute-start) | collective-permute-done | bytes 262176 | tf_op jit(solution)/shard_map/while/body/eval_jaxpr/ppermute | solution.py:11
  185.4 1.9 collective-permute-start
  187.3 9.7 %collective-permute-done = f32[1,4,128,128]{3,2,1,0:T(8,128)S(1)} collective-permute-done((f32[1,4,128,128]{3,2,1,0:T(8,128)S(1)}, f32[1,4,128,128]{3,2,1,0:T(8,128)S(1)}, u32[]{:S(2)}, u32[]{:S(2)}) %collective-permute-start) | collective-permute-done | bytes 262176 | tf_op jit(solution)/shard_map/while/body/eval_jaxpr/ppermute | solution.py:11
  197.1 1.9 collective-permute-start
  199.1 9.7 %collective-permute-done = f32[1,4,128,128]{3,2,1,0:T(8,128)S(1)} collective-permute-done((f32[1,4,128,128]{3,2,1,0:T(8,128)S(1)}, f32[1,4,128,128]{3,2,1,0:T(8,128)S(1)}, u32[]{:S(2)}, u32[]{:S(2)}) %collective-permute-start) | collective-permute-done | bytes 262176 | tf_op jit(solution)/shard_map/while/body/eval_jaxpr/ppermute | solution.py:11
  208.9 1.9 collective-permute-start
  210.8 9.7 %collective-permute-done = f32[1,4,128,128]{3,2,1,0:T(8,128)S(1)} collective-permute-done((f32[1,4,128,128]{3,2,1,0:T(8,128)S(1)}, f32[1,4,128,128]{3,2,1,0:T(8,128)S(1)}, u32[]{:S(2)}, u32[]{:S(2)}) %collective-permute-start) | collective-permute-done | bytes 262176 | tf_op jit(solution)/shard_map/while/body/eval_jaxpr/ppermute | solution.py:11
  220.6 1.9 collective-permute-start
  222.5 9.7 %collective-permute-done = f32[1,4,128,128]{3,2,1,0:T(8,128)S(1)} collective-permute-done((f32[1,4,128,128]{3,2,1,0:T(8,128)S(1)}, f32[1,4,128,128]{3,2,1,0:T(8,128)S(1)}, u32[]{:S(2)}, u32[]{:S(2)}) %collective-permute-start) | collective-permute-done | bytes 262176 | tf_op jit(solution)/shard_map/while/body/eval_jaxpr/ppermute | solution.py:11
  232.3 1.9 collective-permute-start
  234.3 9.7 %collective-permute-done = f32[1,4,128,128]{3,2,1,0:T(8,128)S(1)} collective-permute-done((f32[1,4,128,128]{3,2,1,0:T(8,128)S(1)}, f32[1,4,128,128]{3,2,1,0:T(8,128)S(1)}, u32[]{:S(2)}, u32[]{:S(2)}) %collective-permute-start) | collective-permute-done | bytes 262176 | tf_op jit(solution)/shard_map/while/body/eval_jaxpr/ppermute | solution.py:11
  244.1 1.9 collective-permute-start
  246.0 9.7 %collective-permute-done = f32[1,4,128,128]{3,2,1,0:T(8,128)S(1)} collective-permute-done((f32[1,4,128,128]{3,2,1,0:T(8,128)S(1)}, f32[1,4,128,128]{3,2,1,0:T(8,128)S(1)}, u32[]{:S(2)}, u32[]{:S(2)}) %collective-permute-start) | collective-permute-done | bytes 262176 | tf_op jit(solution)/shard_map/while/body/eval_jaxpr/ppermute | solution.py:11
  255.8 1.9 collective-permute-start
  257.7 9.7 %collective-permute-done = f32[1,4,128,128]{3,2,1,0:T(8,128)S(1)} collective-permute-done((f32[1,4,128,128]{3,2,1,0:T(8,128)S(1)}, f32[1,4,128,128]{3,2,1,0:T(8,128)S(1)}, u32[]{:S(2)}, u32[]{:S(2)}) %collective-permute-start) | collective-permute-done | bytes 262176 | tf_op jit(solution)/shard_map/while/body/eval_jaxpr/ppermute | solution.py:11
  267.5 1.9 collective-permute-start
  269.5 9.7 %collective-permute-done = f32[1,4,128,128]{3,2,1,0:T(8,128)S(1)} collective-permute-done((f32[1,4,128,128]{3,2,1,0:T(8,128)S(1)}, f32[1,4,128,128]{3,2,1,0:T(8,128)S(1)}, u32[]{:S(2)}, u32[]{:S(2)}) %collective-permute-start) | collective-permute-done | bytes 262176 | tf_op jit(solution)/shard_map/while/body/eval_jaxpr/ppermute | solution.py:11
  281.2 9.7 %collective-permute-done = f32[1,4,128,128]{3,2,1,0:T(8,128)S(1)} collective-permute-done((f32[1,4,128,128]{3,2,1,0:T(8,128)S(1)}, f32[1,4,128,128]{3,2,1,0:T(8,128)S(1)}, u32[]{:S(2)}, u32[]{:S(2)}) %collective-permute-start) | collective-permute-done | bytes 262176 | tf_op jit(solution)/shard_map/while/body/eval_jaxpr/ppermute | solution.py:11
  291.0 1.9 collective-permute-start
  292.9 9.7 %collective-permute-done = f32[1,4,128,128]{3,2,1,0:T(8,128)S(1)} collective-permute-done((f32[1,4,128,128]{3,2,1,0:T(8,128)S(1)}, f32[1,4,128,128]{3,2,1,0:T(8,128)S(1)}, u32[]{:S(2)}, u32[]{:S(2)}) %collective-permute-start) | collective-permute-done | bytes 262176 | tf_op jit(solution)/shard_map/while/body/eval_jaxpr/ppermute | solution.py:11
  302.7 1.9 collective-permute-start
  304.7 9.7 %collective-permute-done = f32[1,4,128,128]{3,2,1,0:T(8,128)S(1)} collective-permute-done((f32[1,4,128,128]{3,2,1,0:T(8,128)S(1)}, f32[1,4,128,128]{3,2,1,0:T(8,128)S(1)}, u32[]{:S(2)}, u32[]{:S(2)}) %collective-permute-start) | collective-permute-done | bytes 262176 | tf_op jit(solution)/shard_map/while/body/eval_jaxpr/ppermute | solution.py:11
  316.4 9.7 %collective-permute-done = f32[1,4,128,128]{3,2,1,0:T(8,128)S(1)} collective-permute-done((f32[1,4,128,128]{3,2,1,0:T(8,128)S(1)}, f32[1,4,128,128]{3,2,1,0:T(8,128)S(1)}, u32[]{:S(2)}, u32[]{:S(2)}) %collective-permute-start) | collective-permute-done | bytes 262176 | tf_op jit(solution)/shard_map/while/body/eval_jaxpr/ppermute | solution.py:11
  328.1 9.7 %collective-permute-done = f32[1,4,128,128]{3,2,1,0:T(8,128)S(1)} collective-permute-done((f32[1,4,128,128]{3,2,1,0:T(8,128)S(1)}, f32[1,4,128,128]{3,2,1,0:T(8,128)S(1)}, u32[]{:S(2)}, u32[]{:S(2)}) %collective-permute-start) | collective-permute-done | bytes 262176 | tf_op jit(solution)/shard_map/while/body/eval_jaxpr/ppermute | solution.py:11
  339.9 9.7 %collective-permute-done = f32[1,4,128,128]{3,2,1,0:T(8,128)S(1)} collective-permute-done((f32[1,4,128,128]{3,2,1,0:T(8,128)S(1)}, f32[1,4,128,128]{3,2,1,0:T(8,128)S(1)}, u32[]{:S(2)}, u32[]{:S(2)}) %collective-permute-start) | collective-permute-done | bytes 262176 | tf_op jit(solution)/shard_map/while/body/eval_jaxpr/ppermute | solution.py:11
  351.6 9.7 %collective-permute-done = f32[1,4,128,128]{3,2,1,0:T(8,128)S(1)} collective-permute-done((f32[1,4,128,128]{3,2,1,0:T(8,128)S(1)}, f32[1,4,128,128]{3,2,1,0:T(8,128)S(1)}, u32[]{:S(2)}, u32[]{:S(2)}) %collective-permute-start) | collective-permute-done | bytes 262176 | tf_op jit(solution)/shard_map/while/body/eval_jaxpr/ppermute | solution.py:11
  361.4 1.9 collective-permute-start
  363.4 9.8 %collective-permute-done = f32[1,4,128,128]{3,2,1,0:T(8,128)S(1)} collective-permute-done((f32[1,4,128,128]{3,2,1,0:T(8,128)S(1)}, f32[1,4,128,128]{3,2,1,0:T(8,128)S(1)}, u32[]{:S(2)}, u32[]{:S(2)}) %collective-permute-start) | collective-permute-done | bytes 262176 | tf_op jit(solution)/shard_map/while/body/eval_jaxpr/ppermute | solution.py:11
  373.2 2.3 subtract_maximum_fusion
  375.5 2.4 fusion.1
  377.9 9.5 %fusion.2 = f32[4,1024,128]{1,2,0:T(8,128)} fusion(bf16[1024,4,128]{0,2,1:T(8,128)(2,1)S(1)} %bitcast.32, f32[1024,1024]{1,0:T(8,128)} %fusion.1, f32[1024,1024]{1,0:T(8,128)} %subtract_maximum_fusion, f32[4]{0:T(128)S(1)} %get-tuple-element.98, bf16[1024,4,128]{2,1,0:T(4,128)(2,1)S(1)} %reshape.273, bf16[1024,4,128]{2,1,0:T(4,128)(2,1)S(1)} %reshape.275), kind=kOutput, calls=%fused_computation.7 | convolution fusion | flops 2164260864 | bytes 13631504 | tf_op jit(solution)/shard_map/shij,sjhd->sihd/dot_general | solution.py:32
  387.5 4.1 fusion.3
  391.5 54.0 %psum.7 = f32[1,1024]{1,0:T(1,128)S(1)} all-reduce(f32[1,1024]{1,0:T(1,128)S(1)} %bitcast.33), channel_id=1, replica_groups=mesh['head'=16,'seq'=32] {'head'}, use_global_device_ids=true, to_apply=%region_3.4 | all-reduce | flops 1024 | bytes 8192 | tf_op jit(solution)/shard_map/psum | solution.py:62
  447.4 2.8 multiply_convert_fusion.1
  (84 shorter events, 21.4 us)
Async XLA Ops:
  0.0 4.2 copy-start
  7.4 13.6 %collective-permute-start = (f32[1,4,128,128]{3,2,1,0:T(8,128)S(1)}, f32[1,4,128,128]{3,2,1,0:T(8,128)S(1)}, u32[]{:S(2)}, u32[]{:S(2)}) collective-permute-start(f32[1,4,128,128]{3,2,1,0:T(8,128)S(1)} %fusion.21), channel_id=1, source_target_pairs={{0,1},{1,2},{2,3},{3,4},{4,5},{5,6},{6,7},{7,8},{8,9},{9,10},{10,1... | collective-permute-start | bytes 786440 | tf_op jit(solution)/shard_map/while/body/eval_jaxpr/ppermute | solution.py:11
  21.1 11.6 %collective-permute-start = (f32[1,4,128,128]{3,2,1,0:T(8,128)S(1)}, f32[1,4,128,128]{3,2,1,0:T(8,128)S(1)}, u32[]{:S(2)}, u32[]{:S(2)}) collective-permute-start(f32[1,4,128,128]{3,2,1,0:T(8,128)S(1)} %fusion.21), channel_id=1, source_target_pairs={{0,1},{1,2},{2,3},{3,4},{4,5},{5,6},{6,7},{7,8},{8,9},{9,10},{10,1... | collective-permute-start | bytes 786440 | tf_op jit(solution)/shard_map/while/body/eval_jaxpr/ppermute | solution.py:11
  32.8 11.6 %collective-permute-start = (f32[1,4,128,128]{3,2,1,0:T(8,128)S(1)}, f32[1,4,128,128]{3,2,1,0:T(8,128)S(1)}, u32[]{:S(2)}, u32[]{:S(2)}) collective-permute-start(f32[1,4,128,128]{3,2,1,0:T(8,128)S(1)} %fusion.21), channel_id=1, source_target_pairs={{0,1},{1,2},{2,3},{3,4},{4,5},{5,6},{6,7},{7,8},{8,9},{9,10},{10,1... | collective-permute-start | bytes 786440 | tf_op jit(solution)/shard_map/while/body/eval_jaxpr/ppermute | solution.py:11
  44.6 11.6 %collective-permute-start = (f32[1,4,128,128]{3,2,1,0:T(8,128)S(1)}, f32[1,4,128,128]{3,2,1,0:T(8,128)S(1)}, u32[]{:S(2)}, u32[]{:S(2)}) collective-permute-start(f32[1,4,128,128]{3,2,1,0:T(8,128)S(1)} %fusion.21), channel_id=1, source_target_pairs={{0,1},{1,2},{2,3},{3,4},{4,5},{5,6},{6,7},{7,8},{8,9},{9,10},{10,1... | collective-permute-start | bytes 786440 | tf_op jit(solution)/shard_map/while/body/eval_jaxpr/ppermute | solution.py:11
  56.3 11.6 %collective-permute-start = (f32[1,4,128,128]{3,2,1,0:T(8,128)S(1)}, f32[1,4,128,128]{3,2,1,0:T(8,128)S(1)}, u32[]{:S(2)}, u32[]{:S(2)}) collective-permute-start(f32[1,4,128,128]{3,2,1,0:T(8,128)S(1)} %fusion.21), channel_id=1, source_target_pairs={{0,1},{1,2},{2,3},{3,4},{4,5},{5,6},{6,7},{7,8},{8,9},{9,10},{10,1... | collective-permute-start | bytes 786440 | tf_op jit(solution)/shard_map/while/body/eval_jaxpr/ppermute | solution.py:11
  68.0 11.6 %collective-permute-start = (f32[1,4,128,128]{3,2,1,0:T(8,128)S(1)}, f32[1,4,128,128]{3,2,1,0:T(8,128)S(1)}, u32[]{:S(2)}, u32[]{:S(2)}) collective-permute-start(f32[1,4,128,128]{3,2,1,0:T(8,128)S(1)} %fusion.21), channel_id=1, source_target_pairs={{0,1},{1,2},{2,3},{3,4},{4,5},{5,6},{6,7},{7,8},{8,9},{9,10},{10,1... | collective-permute-start | bytes 786440 | tf_op jit(solution)/shard_map/while/body/eval_jaxpr/ppermute | solution.py:11
  79.8 11.6 %collective-permute-start = (f32[1,4,128,128]{3,2,1,0:T(8,128)S(1)}, f32[1,4,128,128]{3,2,1,0:T(8,128)S(1)}, u32[]{:S(2)}, u32[]{:S(2)}) collective-permute-start(f32[1,4,128,128]{3,2,1,0:T(8,128)S(1)} %fusion.21), channel_id=1, source_target_pairs={{0,1},{1,2},{2,3},{3,4},{4,5},{5,6},{6,7},{7,8},{8,9},{9,10},{10,1... | collective-permute-start | bytes 786440 | tf_op jit(solution)/shard_map/while/body/eval_jaxpr/ppermute | solution.py:11
  91.5 11.6 %collective-permute-start = (f32[1,4,128,128]{3,2,1,0:T(8,128)S(1)}, f32[1,4,128,128]{3,2,1,0:T(8,128)S(1)}, u32[]{:S(2)}, u32[]{:S(2)}) collective-permute-start(f32[1,4,128,128]{3,2,1,0:T(8,128)S(1)} %fusion.21), channel_id=1, source_target_pairs={{0,1},{1,2},{2,3},{3,4},{4,5},{5,6},{6,7},{7,8},{8,9},{9,10},{10,1... | collective-permute-start | bytes 786440 | tf_op jit(solution)/shard_map/while/body/eval_jaxpr/ppermute | solution.py:11
  103.2 11.6 %collective-permute-start = (f32[1,4,128,128]{3,2,1,0:T(8,128)S(1)}, f32[1,4,128,128]{3,2,1,0:T(8,128)S(1)}, u32[]{:S(2)}, u32[]{:S(2)}) collective-permute-start(f32[1,4,128,128]{3,2,1,0:T(8,128)S(1)} %fusion.21), channel_id=1, source_target_pairs={{0,1},{1,2},{2,3},{3,4},{4,5},{5,6},{6,7},{7,8},{8,9},{9,10},{10,1... | collective-permute-start | bytes 786440 | tf_op jit(solution)/shard_map/while/body/eval_jaxpr/ppermute | solution.py:11
  115.0 11.6 %collective-permute-start = (f32[1,4,128,128]{3,2,1,0:T(8,128)S(1)}, f32[1,4,128,128]{3,2,1,0:T(8,128)S(1)}, u32[]{:S(2)}, u32[]{:S(2)}) collective-permute-start(f32[1,4,128,128]{3,2,1,0:T(8,128)S(1)} %fusion.21), channel_id=1, source_target_pairs={{0,1},{1,2},{2,3},{3,4},{4,5},{5,6},{6,7},{7,8},{8,9},{9,10},{10,1... | collective-permute-start | bytes 786440 | tf_op jit(solution)/shard_map/while/body/eval_jaxpr/ppermute | solution.py:11
  126.7 11.6 %collective-permute-start = (f32[1,4,128,128]{3,2,1,0:T(8,128)S(1)}, f32[1,4,128,128]{3,2,1,0:T(8,128)S(1)}, u32[]{:S(2)}, u32[]{:S(2)}) collective-permute-start(f32[1,4,128,128]{3,2,1,0:T(8,128)S(1)} %fusion.21), channel_id=1, source_target_pairs={{0,1},{1,2},{2,3},{3,4},{4,5},{5,6},{6,7},{7,8},{8,9},{9,10},{10,1... | collective-permute-start | bytes 786440 | tf_op jit(solution)/shard_map/while/body/eval_jaxpr/ppermute | solution.py:11
  138.4 11.6 %collective-permute-start = (f32[1,4,128,128]{3,2,1,0:T(8,128)S(1)}, f32[1,4,128,128]{3,2,1,0:T(8,128)S(1)}, u32[]{:S(2)}, u32[]{:S(2)}) collective-permute-start(f32[1,4,128,128]{3,2,1,0:T(8,128)S(1)} %fusion.21), channel_id=1, source_target_pairs={{0,1},{1,2},{2,3},{3,4},{4,5},{5,6},{6,7},{7,8},{8,9},{9,10},{10,1... | collective-permute-start | bytes 786440 | tf_op jit(solution)/shard_map/while/body/eval_jaxpr/ppermute | solution.py:11
  150.2 11.6 %collective-permute-start = (f32[1,4,128,128]{3,2,1,0:T(8,128)S(1)}, f32[1,4,128,128]{3,2,1,0:T(8,128)S(1)}, u32[]{:S(2)}, u32[]{:S(2)}) collective-permute-start(f32[1,4,128,128]{3,2,1,0:T(8,128)S(1)} %fusion.21), channel_id=1, source_target_pairs={{0,1},{1,2},{2,3},{3,4},{4,5},{5,6},{6,7},{7,8},{8,9},{9,10},{10,1... | collective-permute-start | bytes 786440 | tf_op jit(solution)/shard_map/while/body/eval_jaxpr/ppermute | solution.py:11
  161.9 11.6 %collective-permute-start = (f32[1,4,128,128]{3,2,1,0:T(8,128)S(1)}, f32[1,4,128,128]{3,2,1,0:T(8,128)S(1)}, u32[]{:S(2)}, u32[]{:S(2)}) collective-permute-start(f32[1,4,128,128]{3,2,1,0:T(8,128)S(1)} %fusion.21), channel_id=1, source_target_pairs={{0,1},{1,2},{2,3},{3,4},{4,5},{5,6},{6,7},{7,8},{8,9},{9,10},{10,1... | collective-permute-start | bytes 786440 | tf_op jit(solution)/shard_map/while/body/eval_jaxpr/ppermute | solution.py:11
  173.7 11.6 %collective-permute-start = (f32[1,4,128,128]{3,2,1,0:T(8,128)S(1)}, f32[1,4,128,128]{3,2,1,0:T(8,128)S(1)}, u32[]{:S(2)}, u32[]{:S(2)}) collective-permute-start(f32[1,4,128,128]{3,2,1,0:T(8,128)S(1)} %fusion.21), channel_id=1, source_target_pairs={{0,1},{1,2},{2,3},{3,4},{4,5},{5,6},{6,7},{7,8},{8,9},{9,10},{10,1... | collective-permute-start | bytes 786440 | tf_op jit(solution)/shard_map/while/body/eval_jaxpr/ppermute | solution.py:11
  185.4 11.6 %collective-permute-start = (f32[1,4,128,128]{3,2,1,0:T(8,128)S(1)}, f32[1,4,128,128]{3,2,1,0:T(8,128)S(1)}, u32[]{:S(2)}, u32[]{:S(2)}) collective-permute-start(f32[1,4,128,128]{3,2,1,0:T(8,128)S(1)} %fusion.21), channel_id=1, source_target_pairs={{0,1},{1,2},{2,3},{3,4},{4,5},{5,6},{6,7},{7,8},{8,9},{9,10},{10,1... | collective-permute-start | bytes 786440 | tf_op jit(solution)/shard_map/while/body/eval_jaxpr/ppermute | solution.py:11
  197.1 11.6 %collective-permute-start = (f32[1,4,128,128]{3,2,1,0:T(8,128)S(1)}, f32[1,4,128,128]{3,2,1,0:T(8,128)S(1)}, u32[]{:S(2)}, u32[]{:S(2)}) collective-permute-start(f32[1,4,128,128]{3,2,1,0:T(8,128)S(1)} %fusion.21), channel_id=1, source_target_pairs={{0,1},{1,2},{2,3},{3,4},{4,5},{5,6},{6,7},{7,8},{8,9},{9,10},{10,1... | collective-permute-start | bytes 786440 | tf_op jit(solution)/shard_map/while/body/eval_jaxpr/ppermute | solution.py:11
  208.9 11.6 %collective-permute-start = (f32[1,4,128,128]{3,2,1,0:T(8,128)S(1)}, f32[1,4,128,128]{3,2,1,0:T(8,128)S(1)}, u32[]{:S(2)}, u32[]{:S(2)}) collective-permute-start(f32[1,4,128,128]{3,2,1,0:T(8,128)S(1)} %fusion.21), channel_id=1, source_target_pairs={{0,1},{1,2},{2,3},{3,4},{4,5},{5,6},{6,7},{7,8},{8,9},{9,10},{10,1... | collective-permute-start | bytes 786440 | tf_op jit(solution)/shard_map/while/body/eval_jaxpr/ppermute | solution.py:11
  220.6 11.6 %collective-permute-start = (f32[1,4,128,128]{3,2,1,0:T(8,128)S(1)}, f32[1,4,128,128]{3,2,1,0:T(8,128)S(1)}, u32[]{:S(2)}, u32[]{:S(2)}) collective-permute-start(f32[1,4,128,128]{3,2,1,0:T(8,128)S(1)} %fusion.21), channel_id=1, source_target_pairs={{0,1},{1,2},{2,3},{3,4},{4,5},{5,6},{6,7},{7,8},{8,9},{9,10},{10,1... | collective-permute-start | bytes 786440 | tf_op jit(solution)/shard_map/while/body/eval_jaxpr/ppermute | solution.py:11
  232.3 11.6 %collective-permute-start = (f32[1,4,128,128]{3,2,1,0:T(8,128)S(1)}, f32[1,4,128,128]{3,2,1,0:T(8,128)S(1)}, u32[]{:S(2)}, u32[]{:S(2)}) collective-permute-start(f32[1,4,128,128]{3,2,1,0:T(8,128)S(1)} %fusion.21), channel_id=1, source_target_pairs={{0,1},{1,2},{2,3},{3,4},{4,5},{5,6},{6,7},{7,8},{8,9},{9,10},{10,1... | collective-permute-start | bytes 786440 | tf_op jit(solution)/shard_map/while/body/eval_jaxpr/ppermute | solution.py:11
  244.1 11.6 %collective-permute-start = (f32[1,4,128,128]{3,2,1,0:T(8,128)S(1)}, f32[1,4,128,128]{3,2,1,0:T(8,128)S(1)}, u32[]{:S(2)}, u32[]{:S(2)}) collective-permute-start(f32[1,4,128,128]{3,2,1,0:T(8,128)S(1)} %fusion.21), channel_id=1, source_target_pairs={{0,1},{1,2},{2,3},{3,4},{4,5},{5,6},{6,7},{7,8},{8,9},{9,10},{10,1... | collective-permute-start | bytes 786440 | tf_op jit(solution)/shard_map/while/body/eval_jaxpr/ppermute | solution.py:11
  255.8 11.6 %collective-permute-start = (f32[1,4,128,128]{3,2,1,0:T(8,128)S(1)}, f32[1,4,128,128]{3,2,1,0:T(8,128)S(1)}, u32[]{:S(2)}, u32[]{:S(2)}) collective-permute-start(f32[1,4,128,128]{3,2,1,0:T(8,128)S(1)} %fusion.21), channel_id=1, source_target_pairs={{0,1},{1,2},{2,3},{3,4},{4,5},{5,6},{6,7},{7,8},{8,9},{9,10},{10,1... | collective-permute-start | bytes 786440 | tf_op jit(solution)/shard_map/while/body/eval_jaxpr/ppermute | solution.py:11
  267.5 11.6 %collective-permute-start = (f32[1,4,128,128]{3,2,1,0:T(8,128)S(1)}, f32[1,4,128,128]{3,2,1,0:T(8,128)S(1)}, u32[]{:S(2)}, u32[]{:S(2)}) collective-permute-start(f32[1,4,128,128]{3,2,1,0:T(8,128)S(1)} %fusion.21), channel_id=1, source_target_pairs={{0,1},{1,2},{2,3},{3,4},{4,5},{5,6},{6,7},{7,8},{8,9},{9,10},{10,1... | collective-permute-start | bytes 786440 | tf_op jit(solution)/shard_map/while/body/eval_jaxpr/ppermute | solution.py:11
  279.3 11.6 %collective-permute-start = (f32[1,4,128,128]{3,2,1,0:T(8,128)S(1)}, f32[1,4,128,128]{3,2,1,0:T(8,128)S(1)}, u32[]{:S(2)}, u32[]{:S(2)}) collective-permute-start(f32[1,4,128,128]{3,2,1,0:T(8,128)S(1)} %fusion.21), channel_id=1, source_target_pairs={{0,1},{1,2},{2,3},{3,4},{4,5},{5,6},{6,7},{7,8},{8,9},{9,10},{10,1... | collective-permute-start | bytes 786440 | tf_op jit(solution)/shard_map/while/body/eval_jaxpr/ppermute | solution.py:11
  291.0 11.6 %collective-permute-start = (f32[1,4,128,128]{3,2,1,0:T(8,128)S(1)}, f32[1,4,128,128]{3,2,1,0:T(8,128)S(1)}, u32[]{:S(2)}, u32[]{:S(2)}) collective-permute-start(f32[1,4,128,128]{3,2,1,0:T(8,128)S(1)} %fusion.21), channel_id=1, source_target_pairs={{0,1},{1,2},{2,3},{3,4},{4,5},{5,6},{6,7},{7,8},{8,9},{9,10},{10,1... | collective-permute-start | bytes 786440 | tf_op jit(solution)/shard_map/while/body/eval_jaxpr/ppermute | solution.py:11
  302.7 11.6 %collective-permute-start = (f32[1,4,128,128]{3,2,1,0:T(8,128)S(1)}, f32[1,4,128,128]{3,2,1,0:T(8,128)S(1)}, u32[]{:S(2)}, u32[]{:S(2)}) collective-permute-start(f32[1,4,128,128]{3,2,1,0:T(8,128)S(1)} %fusion.21), channel_id=1, source_target_pairs={{0,1},{1,2},{2,3},{3,4},{4,5},{5,6},{6,7},{7,8},{8,9},{9,10},{10,1... | collective-permute-start | bytes 786440 | tf_op jit(solution)/shard_map/while/body/eval_jaxpr/ppermute | solution.py:11
  314.5 11.6 %collective-permute-start = (f32[1,4,128,128]{3,2,1,0:T(8,128)S(1)}, f32[1,4,128,128]{3,2,1,0:T(8,128)S(1)}, u32[]{:S(2)}, u32[]{:S(2)}) collective-permute-start(f32[1,4,128,128]{3,2,1,0:T(8,128)S(1)} %fusion.21), channel_id=1, source_target_pairs={{0,1},{1,2},{2,3},{3,4},{4,5},{5,6},{6,7},{7,8},{8,9},{9,10},{10,1... | collective-permute-start | bytes 786440 | tf_op jit(solution)/shard_map/while/body/eval_jaxpr/ppermute | solution.py:11
  326.2 11.6 %collective-permute-start = (f32[1,4,128,128]{3,2,1,0:T(8,128)S(1)}, f32[1,4,128,128]{3,2,1,0:T(8,128)S(1)}, u32[]{:S(2)}, u32[]{:S(2)}) collective-permute-start(f32[1,4,128,128]{3,2,1,0:T(8,128)S(1)} %fusion.21), channel_id=1, source_target_pairs={{0,1},{1,2},{2,3},{3,4},{4,5},{5,6},{6,7},{7,8},{8,9},{9,10},{10,1... | collective-permute-start | bytes 786440 | tf_op jit(solution)/shard_map/while/body/eval_jaxpr/ppermute | solution.py:11
  337.9 11.6 %collective-permute-start = (f32[1,4,128,128]{3,2,1,0:T(8,128)S(1)}, f32[1,4,128,128]{3,2,1,0:T(8,128)S(1)}, u32[]{:S(2)}, u32[]{:S(2)}) collective-permute-start(f32[1,4,128,128]{3,2,1,0:T(8,128)S(1)} %fusion.21), channel_id=1, source_target_pairs={{0,1},{1,2},{2,3},{3,4},{4,5},{5,6},{6,7},{7,8},{8,9},{9,10},{10,1... | collective-permute-start | bytes 786440 | tf_op jit(solution)/shard_map/while/body/eval_jaxpr/ppermute | solution.py:11
  349.7 11.6 %collective-permute-start = (f32[1,4,128,128]{3,2,1,0:T(8,128)S(1)}, f32[1,4,128,128]{3,2,1,0:T(8,128)S(1)}, u32[]{:S(2)}, u32[]{:S(2)}) collective-permute-start(f32[1,4,128,128]{3,2,1,0:T(8,128)S(1)} %fusion.21), channel_id=1, source_target_pairs={{0,1},{1,2},{2,3},{3,4},{4,5},{5,6},{6,7},{7,8},{8,9},{9,10},{10,1... | collective-permute-start | bytes 786440 | tf_op jit(solution)/shard_map/while/body/eval_jaxpr/ppermute | solution.py:11
  361.4 11.7 %collective-permute-start = (f32[1,4,128,128]{3,2,1,0:T(8,128)S(1)}, f32[1,4,128,128]{3,2,1,0:T(8,128)S(1)}, u32[]{:S(2)}, u32[]{:S(2)}) collective-permute-start(f32[1,4,128,128]{3,2,1,0:T(8,128)S(1)} %fusion.21), channel_id=1, source_target_pairs={{0,1},{1,2},{2,3},{3,4},{4,5},{5,6},{6,7},{7,8},{8,9},{9,10},{10,1... | collective-permute-start | bytes 786440 | tf_op jit(solution)/shard_map/while/body/eval_jaxpr/ppermute | solution.py:11
  373.2 4.8 %copy-start.1 = (bf16[1,1024,512]{1,2,0:T(8,128)(2,1)S(1)}, bf16[1,1024,512]{1,2,0:T(8,128)(2,1)}, u32[]{:S(2)}) copy-start(bf16[1,1024,512]{1,2,0:T(8,128)(2,1)} %copy.14) | copy-start | bytes 3145732
  387.5 59.9 %copy-start.2 = (f32[512]{0:T(512)S(1)}, f32[512]{0:T(512)}, u32[]{:S(2)}) copy-start(f32[512]{0:T(512)} %param.12) | copy-start | bytes 6148
where the time goes:
time: 451 us; the launch traced here: 450 us
  waiting for transfers between devices  302 us (67%)
  starting transfers between devices  59.5 us (13%)
  blocking collectives  54 us (12%)
  matrix products  15.3 us (3%)
  other arithmetic  11.8 us (3%)
  local copies, waits for them, and re-layouts  5.88 us (1%)
    ppermute x31, waiting for transfers between devices, from_behind(): lax.ppermute(shard, axis, [(i, (i + by) % count) for i in range(count)])  302 us
    ppermute x31, starting transfers between devices, from_behind(): lax.ppermute(shard, axis, [(i, (i + by) % count) for i in range(count)])  59.5 us
    psum x1, blocking collectives, body(): sum_squares = lax.psum(squares, 'head')  54 us
    dot_general x1, matrix products, body(): jnp.einsum('shij,sjhd->sihd', weights, value_heads, preferred_element_typ...  9.53 us
  transfers between devices with their start and end apart: 31, of which 31 were waited for; matrix products, arithmetic and copies ran while one was open for 0% of the time, Pallas kernels for 0%

commit v1 on v0

--- a/solution.py
+++ b/solution.py
@@ -59,7 +59,7 @@
     )
     attended = (inner_part + carried_part).reshape(seq_count, block_len, columns)
     squares = jnp.sum(attended * attended, axis=-1)
-    sum_squares = lax.psum(squares, "head")
+    sum_squares = jnp.sum(jax.lax.all_gather(squares, axis_name="head"), axis=0)
     features_all = columns * lax.axis_size("head")
     inv_rms = lax.rsqrt(sum_squares / features_all + epsilon)
     return (attended * inv_rms[..., None] * norm_gain).astype(jnp.bfloat16)

time: 451 us -> 448 us (level)
    psum x1 -> x0, blocking collectives: 54 us -> none  [body(): sum_squares = lax.psum(squares, 'head')]
    all_gather x0 -> x1, blocking collectives: none -> 53.2 us  [body(): sum_squares = jnp.sum(jax.lax.all_gather(squares, axis_name='head'), axis=0)]
where the time goes in v1:
time: 448 us; the launch traced here: 447 us
  waiting for transfers between devices  302 us (67%)
  starting transfers between devices  59.5 us (13%)
  blocking collectives  53.2 us (12%)
  matrix products  14.6 us (3%)
  other arithmetic  10.2 us (2%)
  local copies, waits for them, and re-layouts  6 us (1%)
    ppermute x31, waiting for transfers between devices, from_behind(): lax.ppermute(shard, axis, [(i, (i + by) % count) for i in range(count)])  302 us
    ppermute x31, starting transfers between devices, from_behind(): lax.ppermute(shard, axis, [(i, (i + by) % count) for i in range(count)])  59.5 us
    all_gather x1, blocking collectives, body(): sum_squares = jnp.sum(jax.lax.all_gather(squares, axis_name='head'), axis=0)  53.2 us
    dot_general x1, matrix products, body(): jnp.einsum('shij,sjhd->sihd', weights, value_heads, preferred_element_typ...  9.08 us
  transfers between devices with their start and end apart: 31, of which 31 were waited for; matrix products, arithmetic and copies ran while one was open for 0% of the time, Pallas kernels for 0%

profile of v1, /device:TPU:8, one launch (start us, length us, event | category | flops | bytes accessed | tf_op | source)
XLA Modules:
  0.0 447.4 jit_solution(16749843118698268623)
XLA Ops:
  7.3 365.9 %while.13 = (s32[]{:T(128)}, f32[1,4,128,128]{3,2,1,0:T(8,128)S(1)}, pred[1]{0:T(512)(128)(4,1)}, f32[1,4,1,1]{1,3,2,0:T(1,128)S(1)}, f32[1,4,128,128]{3,2,1,0:T(8,128)S(1)}, /*index=5*/s32[]{:T(128)}, s32[]{:T(128)}) while((s32[]{:T(128)}, f32[1,4,128,128]{3,2,1,0:T(8,128)S(1)}, pred[1]{0:T(512)(128)(4,1)}, ...), condition=%wide.region_1.2_spmd.clone, body=%wide.region_0.1_spmd.clone.sunk | while | flops 262148 | bytes 2359448 | solution.py:54
  7.4 1.9 collective-permute-start
  9.4 11.7 %collective-permute-done = f32[1,4,128,128]{3,2,1,0:T(8,128)S(1)} collective-permute-done((f32[1,4,128,128]{3,2,1,0:T(8,128)S(1)}, f32[1,4,128,128]{3,2,1,0:T(8,128)S(1)}, u32[]{:S(2)}, u32[]{:S(2)}) %collective-permute-start) | collective-permute-done | bytes 262176 | tf_op jit(solution)/shard_map/while/body/eval_jaxpr/ppermute | solution.py:11
  21.2 1.9 collective-permute-start
  23.1 9.7 %collective-permute-done = f32[1,4,128,128]{3,2,1,0:T(8,128)S(1)} collective-permute-done((f32[1,4,128,128]{3,2,1,0:T(8,128)S(1)}, f32[1,4,128,128]{3,2,1,0:T(8,128)S(1)}, u32[]{:S(2)}, u32[]{:S(2)}) %collective-permute-start) | collective-permute-done | bytes 262176 | tf_op jit(solution)/shard_map/while/body/eval_jaxpr/ppermute | solution.py:11
  32.9 1.9 collective-permute-start
  34.8 9.7 %collective-permute-done = f32[1,4,128,128]{3,2,1,0:T(8,128)S(1)} collective-permute-done((f32[1,4,128,128]{3,2,1,0:T(8,128)S(1)}, f32[1,4,128,128]{3,2,1,0:T(8,128)S(1)}, u32[]{:S(2)}, u32[]{:S(2)}) %collective-permute-start) | collective-permute-done | bytes 262176 | tf_op jit(solution)/shard_map/while/body/eval_jaxpr/ppermute | solution.py:11
  44.6 1.9 collective-permute-start
  46.6 9.7 %collective-permute-done = f32[1,4,128,128]{3,2,1,0:T(8,128)S(1)} collective-permute-done((f32[1,4,128,128]{3,2,1,0:T(8,128)S(1)}, f32[1,4,128,128]{3,2,1,0:T(8,128)S(1)}, u32[]{:S(2)}, u32[]{:S(2)}) %collective-permute-start) | collective-permute-done | bytes 262176 | tf_op jit(solution)/shard_map/while/body/eval_jaxpr/ppermute | solution.py:11
  56.4 1.9 collective-permute-start
  58.3 9.7 %collective-permute-done = f32[1,4,128,128]{3,2,1,0:T(8,128)S(1)} collective-permute-done((f32[1,4,128,128]{3,2,1,0:T(8,128)S(1)}, f32[1,4,128,128]{3,2,1,0:T(8,128)S(1)}, u32[]{:S(2)}, u32[]{:S(2)}) %collective-permute-start) | collective-permute-done | bytes 262176 | tf_op jit(solution)/shard_map/while/body/eval_jaxpr/ppermute | solution.py:11
  68.1 1.9 collective-permute-start
  70.0 9.7 %collective-permute-done = f32[1,4,128,128]{3,2,1,0:T(8,128)S(1)} collective-permute-done((f32[1,4,128,128]{3,2,1,0:T(8,128)S(1)}, f32[1,4,128,128]{3,2,1,0:T(8,128)S(1)}, u32[]{:S(2)}, u32[]{:S(2)}) %collective-permute-start) | collective-permute-done | bytes 262176 | tf_op jit(solution)/shard_map/while/body/eval_jaxpr/ppermute | solution.py:11
  79.8 1.9 collective-permute-start
  81.8 9.7 %collective-permute-done = f32[1,4,128,128]{3,2,1,0:T(8,128)S(1)} collective-permute-done((f32[1,4,128,128]{3,2,1,0:T(8,128)S(1)}, f32[1,4,128,128]{3,2,1,0:T(8,128)S(1)}, u32[]{:S(2)}, u32[]{:S(2)}) %collective-permute-start) | collective-permute-done | bytes 262176 | tf_op jit(solution)/shard_map/while/body/eval_jaxpr/ppermute | solution.py:11
  91.6 1.9 collective-permute-start
  93.5 9.7 %collective-permute-done = f32[1,4,128,128]{3,2,1,0:T(8,128)S(1)} collective-permute-done((f32[1,4,128,128]{3,2,1,0:T(8,128)S(1)}, f32[1,4,128,128]{3,2,1,0:T(8,128)S(1)}, u32[]{:S(2)}, u32[]{:S(2)}) %collective-permute-start) | collective-permute-done | bytes 262176 | tf_op jit(solution)/shard_map/while/body/eval_jaxpr/ppermute | solution.py:11
  103.3 1.9 collective-permute-start
  105.2 9.7 %collective-permute-done = f32[1,4,128,128]{3,2,1,0:T(8,128)S(1)} collective-permute-done((f32[1,4,128,128]{3,2,1,0:T(8,128)S(1)}, f32[1,4,128,128]{3,2,1,0:T(8,128)S(1)}, u32[]{:S(2)}, u32[]{:S(2)}) %collective-permute-start) | collective-permute-done | bytes 262176 | tf_op jit(solution)/shard_map/while/body/eval_jaxpr/ppermute | solution.py:11
  115.0 1.9 collective-permute-start
  117.0 9.7 %collective-permute-done = f32[1,4,128,128]{3,2,1,0:T(8,128)S(1)} collective-permute-done((f32[1,4,128,128]{3,2,1,0:T(8,128)S(1)}, f32[1,4,128,128]{3,2,1,0:T(8,128)S(1)}, u32[]{:S(2)}, u32[]{:S(2)}) %collective-permute-start) | collective-permute-done | bytes 262176 | tf_op jit(solution)/shard_map/while/body/eval_jaxpr/ppermute | solution.py:11
  126.8 1.9 collective-permute-start
  128.7 9.7 %collective-permute-done = f32[1,4,128,128]{3,2,1,0:T(8,128)S(1)} collective-permute-done((f32[1,4,128,128]{3,2,1,0:T(8,128)S(1)}, f32[1,4,128,128]{3,2,1,0:T(8,128)S(1)}, u32[]{:S(2)}, u32[]{:S(2)}) %collective-permute-start) | collective-permute-done | bytes 262176 | tf_op jit(solution)/shard_map/while/body/eval_jaxpr/ppermute | solution.py:11
  138.5 1.9 collective-permute-start
  140.4 9.7 %collective-permute-done = f32[1,4,128,128]{3,2,1,0:T(8,128)S(1)} collective-permute-done((f32[1,4,128,128]{3,2,1,0:T(8,128)S(1)}, f32[1,4,128,128]{3,2,1,0:T(8,128)S(1)}, u32[]{:S(2)}, u32[]{:S(2)}) %collective-permute-start) | collective-permute-done | bytes 262176 | tf_op jit(solution)/shard_map/while/body/eval_jaxpr/ppermute | solution.py:11
  150.2 1.9 collective-permute-start
  152.2 9.7 %collective-permute-done = f32[1,4,128,128]{3,2,1,0:T(8,128)S(1)} collective-permute-done((f32[1,4,128,128]{3,2,1,0:T(8,128)S(1)}, f32[1,4,128,128]{3,2,1,0:T(8,128)S(1)}, u32[]{:S(2)}, u32[]{:S(2)}) %collective-permute-start) | collective-permute-done | bytes 262176 | tf_op jit(solution)/shard_map/while/body/eval_jaxpr/ppermute | solution.py:11
  162.0 1.9 collective-permute-start
  163.9 9.7 %collective-permute-done = f32[1,4,128,128]{3,2,1,0:T(8,128)S(1)} collective-permute-done((f32[1,4,128,128]{3,2,1,0:T(8,128)S(1)}, f32[1,4,128,128]{3,2,1,0:T(8,128)S(1)}, u32[]{:S(2)}, u32[]{:S(2)}) %collective-permute-start) | collective-permute-done | bytes 262176 | tf_op jit(solution)/shard_map/while/body/eval_jaxpr/ppermute | solution.py:11
  173.7 1.9 collective-permute-start
  175.6 9.7 %collective-permute-done = f32[1,4,128,128]{3,2,1,0:T(8,128)S(1)} collective-permute-done((f32[1,4,128,128]{3,2,1,0:T(8,128)S(1)}, f32[1,4,128,128]{3,2,1,0:T(8,128)S(1)}, u32[]{:S(2)}, u32[]{:S(2)}) %collective-permute-start) | collective-permute-done | bytes 262176 | tf_op jit(solution)/shard_map/while/body/eval_jaxpr/ppermute | solution.py:11
  185.4 1.9 collective-permute-start
  187.4 9.7 %collective-permute-done = f32[1,4,128,128]{3,2,1,0:T(8,128)S(1)} collective-permute-done((f32[1,4,128,128]{3,2,1,0:T(8,128)S(1)}, f32[1,4,128,128]{3,2,1,0:T(8,128)S(1)}, u32[]{:S(2)}, u32[]{:S(2)}) %collective-permute-start) | collective-permute-done | bytes 262176 | tf_op jit(solution)/shard_map/while/body/eval_jaxpr/ppermute | solution.py:11
  197.2 1.9 collective-permute-start
  199.1 9.7 %collective-permute-done = f32[1,4,128,128]{3,2,1,0:T(8,128)S(1)} collective-permute-done((f32[1,4,128,128]{3,2,1,0:T(8,128)S(1)}, f32[1,4,128,128]{3,2,1,0:T(8,128)S(1)}, u32[]{:S(2)}, u32[]{:S(2)}) %collective-permute-start) | collective-permute-done | bytes 262176 | tf_op jit(solution)/shard_map/while/body/eval_jaxpr/ppermute | solution.py:11
  208.9 1.9 collective-permute-start
  210.9 9.7 %collective-permute-done = f32[1,4,128,128]{3,2,1,0:T(8,128)S(1)} collective-permute-done((f32[1,4,128,128]{3,2,1,0:T(8,128)S(1)}, f32[1,4,128,128]{3,2,1,0:T(8,128)S(1)}, u32[]{:S(2)}, u32[]{:S(2)}) %collective-permute-start) | collective-permute-done | bytes 262176 | tf_op jit(solution)/shard_map/while/body/eval_jaxpr/ppermute | solution.py:11
  220.7 1.9 collective-permute-start
  222.6 9.7 %collective-permute-done = f32[1,4,128,128]{3,2,1,0:T(8,128)S(1)} collective-permute-done((f32[1,4,128,128]{3,2,1,0:T(8,128)S(1)}, f32[1,4,128,128]{3,2,1,0:T(8,128)S(1)}, u32[]{:S(2)}, u32[]{:S(2)}) %collective-permute-start) | collective-permute-done | bytes 262176 | tf_op jit(solution)/shard_map/while/body/eval_jaxpr/ppermute | solution.py:11
  232.4 1.9 collective-permute-start
  234.3 9.7 %collective-permute-done = f32[1,4,128,128]{3,2,1,0:T(8,128)S(1)} collective-permute-done((f32[1,4,128,128]{3,2,1,0:T(8,128)S(1)}, f32[1,4,128,128]{3,2,1,0:T(8,128)S(1)}, u32[]{:S(2)}, u32[]{:S(2)}) %collective-permute-start) | collective-permute-done | bytes 262176 | tf_op jit(solution)/shard_map/while/body/eval_jaxpr/ppermute | solution.py:11
  244.1 1.9 collective-permute-start
  246.1 9.7 %collective-permute-done = f32[1,4,128,128]{3,2,1,0:T(8,128)S(1)} collective-permute-done((f32[1,4,128,128]{3,2,1,0:T(8,128)S(1)}, f32[1,4,128,128]{3,2,1,0:T(8,128)S(1)}, u32[]{:S(2)}, u32[]{:S(2)}) %collective-permute-start) | collective-permute-done | bytes 262176 | tf_op jit(solution)/shard_map/while/body/eval_jaxpr/ppermute | solution.py:11
  255.9 1.9 collective-permute-start
  257.8 9.7 %collective-permute-done = f32[1,4,128,128]{3,2,1,0:T(8,128)S(1)} collective-permute-done((f32[1,4,128,128]{3,2,1,0:T(8,128)S(1)}, f32[1,4,128,128]{3,2,1,0:T(8,128)S(1)}, u32[]{:S(2)}, u32[]{:S(2)}) %collective-permute-start) | collective-permute-done | bytes 262176 | tf_op jit(solution)/shard_map/while/body/eval_jaxpr/ppermute | solution.py:11
  267.6 1.9 collective-permute-start
  269.5 9.7 %collective-permute-done = f32[1,4,128,128]{3,2,1,0:T(8,128)S(1)} collective-permute-done((f32[1,4,128,128]{3,2,1,0:T(8,128)S(1)}, f32[1,4,128,128]{3,2,1,0:T(8,128)S(1)}, u32[]{:S(2)}, u32[]{:S(2)}) %collective-permute-start) | collective-permute-done | bytes 262176 | tf_op jit(solution)/shard_map/while/body/eval_jaxpr/ppermute | solution.py:11
  279.3 1.9 collective-permute-start
  281.3 9.7 %collective-permute-done = f32[1,4,128,128]{3,2,1,0:T(8,128)S(1)} collective-permute-done((f32[1,4,128,128]{3,2,1,0:T(8,128)S(1)}, f32[1,4,128,128]{3,2,1,0:T(8,128)S(1)}, u32[]{:S(2)}, u32[]{:S(2)}) %collective-permute-start) | collective-permute-done | bytes 262176 | tf_op jit(solution)/shard_map/while/body/eval_jaxpr/ppermute | solution.py:11
  291.1 1.9 collective-permute-start
  293.0 9.7 %collective-permute-done = f32[1,4,128,128]{3,2,1,0:T(8,128)S(1)} collective-permute-done((f32[1,4,128,128]{3,2,1,0:T(8,128)S(1)}, f32[1,4,128,128]{3,2,1,0:T(8,128)S(1)}, u32[]{:S(2)}, u32[]{:S(2)}) %collective-permute-start) | collective-permute-done | bytes 262176 | tf_op jit(solution)/shard_map/while/body/eval_jaxpr/ppermute | solution.py:11
  304.7 9.7 %collective-permute-done = f32[1,4,128,128]{3,2,1,0:T(8,128)S(1)} collective-permute-done((f32[1,4,128,128]{3,2,1,0:T(8,128)S(1)}, f32[1,4,128,128]{3,2,1,0:T(8,128)S(1)}, u32[]{:S(2)}, u32[]{:S(2)}) %collective-permute-start) | collective-permute-done | bytes 262176 | tf_op jit(solution)/shard_map/while/body/eval_jaxpr/ppermute | solution.py:11
  316.5 9.7 %collective-permute-done = f32[1,4,128,128]{3,2,1,0:T(8,128)S(1)} collective-permute-done((f32[1,4,128,128]{3,2,1,0:T(8,128)S(1)}, f32[1,4,128,128]{3,2,1,0:T(8,128)S(1)}, u32[]{:S(2)}, u32[]{:S(2)}) %collective-permute-start) | collective-permute-done | bytes 262176 | tf_op jit(solution)/shard_map/while/body/eval_jaxpr/ppermute | solution.py:11
  328.2 9.7 %collective-permute-done = f32[1,4,128,128]{3,2,1,0:T(8,128)S(1)} collective-permute-done((f32[1,4,128,128]{3,2,1,0:T(8,128)S(1)}, f32[1,4,128,128]{3,2,1,0:T(8,128)S(1)}, u32[]{:S(2)}, u32[]{:S(2)}) %collective-permute-start) | collective-permute-done | bytes 262176 | tf_op jit(solution)/shard_map/while/body/eval_jaxpr/ppermute | solution.py:11
  338.0 1.9 collective-permute-start
  339.9 9.7 %collective-permute-done = f32[1,4,128,128]{3,2,1,0:T(8,128)S(1)} collective-permute-done((f32[1,4,128,128]{3,2,1,0:T(8,128)S(1)}, f32[1,4,128,128]{3,2,1,0:T(8,128)S(1)}, u32[]{:S(2)}, u32[]{:S(2)}) %collective-permute-start) | collective-permute-done | bytes 262176 | tf_op jit(solution)/shard_map/while/body/eval_jaxpr/ppermute | solution.py:11
  349.7 1.9 collective-permute-start
  351.7 9.7 %collective-permute-done = f32[1,4,128,128]{3,2,1,0:T(8,128)S(1)} collective-permute-done((f32[1,4,128,128]{3,2,1,0:T(8,128)S(1)}, f32[1,4,128,128]{3,2,1,0:T(8,128)S(1)}, u32[]{:S(2)}, u32[]{:S(2)}) %collective-permute-start) | collective-permute-done | bytes 262176 | tf_op jit(solution)/shard_map/while/body/eval_jaxpr/ppermute | solution.py:11
  363.4 9.8 %collective-permute-done = f32[1,4,128,128]{3,2,1,0:T(8,128)S(1)} collective-permute-done((f32[1,4,128,128]{3,2,1,0:T(8,128)S(1)}, f32[1,4,128,128]{3,2,1,0:T(8,128)S(1)}, u32[]{:S(2)}, u32[]{:S(2)}) %collective-permute-start) | collective-permute-done | bytes 262176 | tf_op jit(solution)/shard_map/while/body/eval_jaxpr/ppermute | solution.py:11
  373.2 2.3 subtract_maximum_fusion
  375.5 2.4 fusion.1
  378.0 9.1 %fusion.2 = f32[4,1024,128]{1,2,0:T(8,128)S(1)} fusion(bf16[1024,4,128]{0,2,1:T(8,128)(2,1)} %bitcast.30, f32[1024,1024]{1,0:T(8,128)} %fusion.1, f32[1024,1024]{1,0:T(8,128)} %subtract_maximum_fusion, f32[4]{0:T(128)S(1)} %get-tuple-element.98, bf16[1024,4,128]{2,1,0:T(4,128)(2,1)} %copy-done.1, bf16[1024,4,128]{2,1,0:T(4,128)(2,1)S(1)} %reshape.279), kind=kOutput, calls=%fused_computation.7 | convolution fusion | flops 2164260864 | bytes 13631504 | tf_op jit(solution)/shard_map/shij,sjhd->sihd/dot_general | solution.py:32
  387.1 3.8 fusion.3
  392.8 53.2 %all-gather = f32[16384]{0:T(1024)S(1)} all-gather(f32[1024]{0:T(1024)S(1)} %get-tuple-element.99), channel_id=2, replica_groups=mesh['head'=16,'seq'=32] {'head'}, dimensions={0}, use_global_device_ids=true | all-gather | bytes 69632 | tf_op jit(solution)/shard_map/all_gather | solution.py:62
  (86 shorter events, 20.8 us)
Async XLA Ops:
  0.0 4.2 copy-start
  4.3 3.1 copy-start.1
  7.4 13.6 %collective-permute-start = (f32[1,4,128,128]{3,2,1,0:T(8,128)S(1)}, f32[1,4,128,128]{3,2,1,0:T(8,128)S(1)}, u32[]{:S(2)}, u32[]{:S(2)}) collective-permute-start(f32[1,4,128,128]{3,2,1,0:T(8,128)S(1)} %fusion.21), channel_id=1, source_target_pairs={{0,1},{1,2},{2,3},{3,4},{4,5},{5,6},{6,7},{7,8},{8,9},{9,10},{10,1... | collective-permute-start | bytes 786440 | tf_op jit(solution)/shard_map/while/body/eval_jaxpr/ppermute | solution.py:11
  21.2 11.6 %collective-permute-start = (f32[1,4,128,128]{3,2,1,0:T(8,128)S(1)}, f32[1,4,128,128]{3,2,1,0:T(8,128)S(1)}, u32[]{:S(2)}, u32[]{:S(2)}) collective-permute-start(f32[1,4,128,128]{3,2,1,0:T(8,128)S(1)} %fusion.21), channel_id=1, source_target_pairs={{0,1},{1,2},{2,3},{3,4},{4,5},{5,6},{6,7},{7,8},{8,9},{9,10},{10,1... | collective-permute-start | bytes 786440 | tf_op jit(solution)/shard_map/while/body/eval_jaxpr/ppermute | solution.py:11
  32.9 11.6 %collective-permute-start = (f32[1,4,128,128]{3,2,1,0:T(8,128)S(1)}, f32[1,4,128,128]{3,2,1,0:T(8,128)S(1)}, u32[]{:S(2)}, u32[]{:S(2)}) collective-permute-start(f32[1,4,128,128]{3,2,1,0:T(8,128)S(1)} %fusion.21), channel_id=1, source_target_pairs={{0,1},{1,2},{2,3},{3,4},{4,5},{5,6},{6,7},{7,8},{8,9},{9,10},{10,1... | collective-permute-start | bytes 786440 | tf_op jit(solution)/shard_map/while/body/eval_jaxpr/ppermute | solution.py:11
  44.6 11.6 %collective-permute-start = (f32[1,4,128,128]{3,2,1,0:T(8,128)S(1)}, f32[1,4,128,128]{3,2,1,0:T(8,128)S(1)}, u32[]{:S(2)}, u32[]{:S(2)}) collective-permute-start(f32[1,4,128,128]{3,2,1,0:T(8,128)S(1)} %fusion.21), channel_id=1, source_target_pairs={{0,1},{1,2},{2,3},{3,4},{4,5},{5,6},{6,7},{7,8},{8,9},{9,10},{10,1... | collective-permute-start | bytes 786440 | tf_op jit(solution)/shard_map/while/body/eval_jaxpr/ppermute | solution.py:11
  56.4 11.6 %collective-permute-start = (f32[1,4,128,128]{3,2,1,0:T(8,128)S(1)}, f32[1,4,128,128]{3,2,1,0:T(8,128)S(1)}, u32[]{:S(2)}, u32[]{:S(2)}) collective-permute-start(f32[1,4,128,128]{3,2,1,0:T(8,128)S(1)} %fusion.21), channel_id=1, source_target_pairs={{0,1},{1,2},{2,3},{3,4},{4,5},{5,6},{6,7},{7,8},{8,9},{9,10},{10,1... | collective-permute-start | bytes 786440 | tf_op jit(solution)/shard_map/while/body/eval_jaxpr/ppermute | solution.py:11
  68.1 11.6 %collective-permute-start = (f32[1,4,128,128]{3,2,1,0:T(8,128)S(1)}, f32[1,4,128,128]{3,2,1,0:T(8,128)S(1)}, u32[]{:S(2)}, u32[]{:S(2)}) collective-permute-start(f32[1,4,128,128]{3,2,1,0:T(8,128)S(1)} %fusion.21), channel_id=1, source_target_pairs={{0,1},{1,2},{2,3},{3,4},{4,5},{5,6},{6,7},{7,8},{8,9},{9,10},{10,1... | collective-permute-start | bytes 786440 | tf_op jit(solution)/shard_map/while/body/eval_jaxpr/ppermute | solution.py:11
  79.8 11.6 %collective-permute-start = (f32[1,4,128,128]{3,2,1,0:T(8,128)S(1)}, f32[1,4,128,128]{3,2,1,0:T(8,128)S(1)}, u32[]{:S(2)}, u32[]{:S(2)}) collective-permute-start(f32[1,4,128,128]{3,2,1,0:T(8,128)S(1)} %fusion.21), channel_id=1, source_target_pairs={{0,1},{1,2},{2,3},{3,4},{4,5},{5,6},{6,7},{7,8},{8,9},{9,10},{10,1... | collective-permute-start | bytes 786440 | tf_op jit(solution)/shard_map/while/body/eval_jaxpr/ppermute | solution.py:11
  91.6 11.6 %collective-permute-start = (f32[1,4,128,128]{3,2,1,0:T(8,128)S(1)}, f32[1,4,128,128]{3,2,1,0:T(8,128)S(1)}, u32[]{:S(2)}, u32[]{:S(2)}) collective-permute-start(f32[1,4,128,128]{3,2,1,0:T(8,128)S(1)} %fusion.21), channel_id=1, source_target_pairs={{0,1},{1,2},{2,3},{3,4},{4,5},{5,6},{6,7},{7,8},{8,9},{9,10},{10,1... | collective-permute-start | bytes 786440 | tf_op jit(solution)/shard_map/while/body/eval_jaxpr/ppermute | solution.py:11
  103.3 11.6 %collective-permute-start = (f32[1,4,128,128]{3,2,1,0:T(8,128)S(1)}, f32[1,4,128,128]{3,2,1,0:T(8,128)S(1)}, u32[]{:S(2)}, u32[]{:S(2)}) collective-permute-start(f32[1,4,128,128]{3,2,1,0:T(8,128)S(1)} %fusion.21), channel_id=1, source_target_pairs={{0,1},{1,2},{2,3},{3,4},{4,5},{5,6},{6,7},{7,8},{8,9},{9,10},{10,1... | collective-permute-start | bytes 786440 | tf_op jit(solution)/shard_map/while/body/eval_jaxpr/ppermute | solution.py:11
  115.0 11.6 %collective-permute-start = (f32[1,4,128,128]{3,2,1,0:T(8,128)S(1)}, f32[1,4,128,128]{3,2,1,0:T(8,128)S(1)}, u32[]{:S(2)}, u32[]{:S(2)}) collective-permute-start(f32[1,4,128,128]{3,2,1,0:T(8,128)S(1)} %fusion.21), channel_id=1, source_target_pairs={{0,1},{1,2},{2,3},{3,4},{4,5},{5,6},{6,7},{7,8},{8,9},{9,10},{10,1... | collective-permute-start | bytes 786440 | tf_op jit(solution)/shard_map/while/body/eval_jaxpr/ppermute | solution.py:11
  126.8 11.6 %collective-permute-start = (f32[1,4,128,128]{3,2,1,0:T(8,128)S(1)}, f32[1,4,128,128]{3,2,1,0:T(8,128)S(1)}, u32[]{:S(2)}, u32[]{:S(2)}) collective-permute-start(f32[1,4,128,128]{3,2,1,0:T(8,128)S(1)} %fusion.21), channel_id=1, source_target_pairs={{0,1},{1,2},{2,3},{3,4},{4,5},{5,6},{6,7},{7,8},{8,9},{9,10},{10,1... | collective-permute-start | bytes 786440 | tf_op jit(solution)/shard_map/while/body/eval_jaxpr/ppermute | solution.py:11
  138.5 11.6 %collective-permute-start = (f32[1,4,128,128]{3,2,1,0:T(8,128)S(1)}, f32[1,4,128,128]{3,2,1,0:T(8,128)S(1)}, u32[]{:S(2)}, u32[]{:S(2)}) collective-permute-start(f32[1,4,128,128]{3,2,1,0:T(8,128)S(1)} %fusion.21), channel_id=1, source_target_pairs={{0,1},{1,2},{2,3},{3,4},{4,5},{5,6},{6,7},{7,8},{8,9},{9,10},{10,1... | collective-permute-start | bytes 786440 | tf_op jit(solution)/shard_map/while/body/eval_jaxpr/ppermute | solution.py:11
  150.2 11.6 %collective-permute-start = (f32[1,4,128,128]{3,2,1,0:T(8,128)S(1)}, f32[1,4,128,128]{3,2,1,0:T(8,128)S(1)}, u32[]{:S(2)}, u32[]{:S(2)}) collective-permute-start(f32[1,4,128,128]{3,2,1,0:T(8,128)S(1)} %fusion.21), channel_id=1, source_target_pairs={{0,1},{1,2},{2,3},{3,4},{4,5},{5,6},{6,7},{7,8},{8,9},{9,10},{10,1... | collective-permute-start | bytes 786440 | tf_op jit(solution)/shard_map/while/body/eval_jaxpr/ppermute | solution.py:11
  162.0 11.6 %collective-permute-start = (f32[1,4,128,128]{3,2,1,0:T(8,128)S(1)}, f32[1,4,128,128]{3,2,1,0:T(8,128)S(1)}, u32[]{:S(2)}, u32[]{:S(2)}) collective-permute-start(f32[1,4,128,128]{3,2,1,0:T(8,128)S(1)} %fusion.21), channel_id=1, source_target_pairs={{0,1},{1,2},{2,3},{3,4},{4,5},{5,6},{6,7},{7,8},{8,9},{9,10},{10,1... | collective-permute-start | bytes 786440 | tf_op jit(solution)/shard_map/while/body/eval_jaxpr/ppermute | solution.py:11
  173.7 11.6 %collective-permute-start = (f32[1,4,128,128]{3,2,1,0:T(8,128)S(1)}, f32[1,4,128,128]{3,2,1,0:T(8,128)S(1)}, u32[]{:S(2)}, u32[]{:S(2)}) collective-permute-start(f32[1,4,128,128]{3,2,1,0:T(8,128)S(1)} %fusion.21), channel_id=1, source_target_pairs={{0,1},{1,2},{2,3},{3,4},{4,5},{5,6},{6,7},{7,8},{8,9},{9,10},{10,1... | collective-permute-start | bytes 786440 | tf_op jit(solution)/shard_map/while/body/eval_jaxpr/ppermute | solution.py:11
  185.4 11.6 %collective-permute-start = (f32[1,4,128,128]{3,2,1,0:T(8,128)S(1)}, f32[1,4,128,128]{3,2,1,0:T(8,128)S(1)}, u32[]{:S(2)}, u32[]{:S(2)}) collective-permute-start(f32[1,4,128,128]{3,2,1,0:T(8,128)S(1)} %fusion.21), channel_id=1, source_target_pairs={{0,1},{1,2},{2,3},{3,4},{4,5},{5,6},{6,7},{7,8},{8,9},{9,10},{10,1... | collective-permute-start | bytes 786440 | tf_op jit(solution)/shard_map/while/body/eval_jaxpr/ppermute | solution.py:11
  197.2 11.6 %collective-permute-start = (f32[1,4,128,128]{3,2,1,0:T(8,128)S(1)}, f32[1,4,128,128]{3,2,1,0:T(8,128)S(1)}, u32[]{:S(2)}, u32[]{:S(2)}) collective-permute-start(f32[1,4,128,128]{3,2,1,0:T(8,128)S(1)} %fusion.21), channel_id=1, source_target_pairs={{0,1},{1,2},{2,3},{3,4},{4,5},{5,6},{6,7},{7,8},{8,9},{9,10},{10,1... | collective-permute-start | bytes 786440 | tf_op jit(solution)/shard_map/while/body/eval_jaxpr/ppermute | solution.py:11
  208.9 11.6 %collective-permute-start = (f32[1,4,128,128]{3,2,1,0:T(8,128)S(1)}, f32[1,4,128,128]{3,2,1,0:T(8,128)S(1)}, u32[]{:S(2)}, u32[]{:S(2)}) collective-permute-start(f32[1,4,128,128]{3,2,1,0:T(8,128)S(1)} %fusion.21), channel_id=1, source_target_pairs={{0,1},{1,2},{2,3},{3,4},{4,5},{5,6},{6,7},{7,8},{8,9},{9,10},{10,1... | collective-permute-start | bytes 786440 | tf_op jit(solution)/shard_map/while/body/eval_jaxpr/ppermute | solution.py:11
  220.7 11.6 %collective-permute-start = (f32[1,4,128,128]{3,2,1,0:T(8,128)S(1)}, f32[1,4,128,128]{3,2,1,0:T(8,128)S(1)}, u32[]{:S(2)}, u32[]{:S(2)}) collective-permute-start(f32[1,4,128,128]{3,2,1,0:T(8,128)S(1)} %fusion.21), channel_id=1, source_target_pairs={{0,1},{1,2},{2,3},{3,4},{4,5},{5,6},{6,7},{7,8},{8,9},{9,10},{10,1... | collective-permute-start | bytes 786440 | tf_op jit(solution)/shard_map/while/body/eval_jaxpr/ppermute | solution.py:11
  232.4 11.6 %collective-permute-start = (f32[1,4,128,128]{3,2,1,0:T(8,128)S(1)}, f32[1,4,128,128]{3,2,1,0:T(8,128)S(1)}, u32[]{:S(2)}, u32[]{:S(2)}) collective-permute-start(f32[1,4,128,128]{3,2,1,0:T(8,128)S(1)} %fusion.21), channel_id=1, source_target_pairs={{0,1},{1,2},{2,3},{3,4},{4,5},{5,6},{6,7},{7,8},{8,9},{9,10},{10,1... | collective-permute-start | bytes 786440 | tf_op jit(solution)/shard_map/while/body/eval_jaxpr/ppermute | solution.py:11
  244.1 11.6 %collective-permute-start = (f32[1,4,128,128]{3,2,1,0:T(8,128)S(1)}, f32[1,4,128,128]{3,2,1,0:T(8,128)S(1)}, u32[]{:S(2)}, u32[]{:S(2)}) collective-permute-start(f32[1,4,128,128]{3,2,1,0:T(8,128)S(1)} %fusion.21), channel_id=1, source_target_pairs={{0,1},{1,2},{2,3},{3,4},{4,5},{5,6},{6,7},{7,8},{8,9},{9,10},{10,1... | collective-permute-start | bytes 786440 | tf_op jit(solution)/shard_map/while/body/eval_jaxpr/ppermute | solution.py:11
  255.9 11.6 %collective-permute-start = (f32[1,4,128,128]{3,2,1,0:T(8,128)S(1)}, f32[1,4,128,128]{3,2,1,0:T(8,128)S(1)}, u32[]{:S(2)}, u32[]{:S(2)}) collective-permute-start(f32[1,4,128,128]{3,2,1,0:T(8,128)S(1)} %fusion.21), channel_id=1, source_target_pairs={{0,1},{1,2},{2,3},{3,4},{4,5},{5,6},{6,7},{7,8},{8,9},{9,10},{10,1... | collective-permute-start | bytes 786440 | tf_op jit(solution)/shard_map/while/body/eval_jaxpr/ppermute | solution.py:11
  267.6 11.6 %collective-permute-start = (f32[1,4,128,128]{3,2,1,0:T(8,128)S(1)}, f32[1,4,128,128]{3,2,1,0:T(8,128)S(1)}, u32[]{:S(2)}, u32[]{:S(2)}) collective-permute-start(f32[1,4,128,128]{3,2,1,0:T(8,128)S(1)} %fusion.21), channel_id=1, source_target_pairs={{0,1},{1,2},{2,3},{3,4},{4,5},{5,6},{6,7},{7,8},{8,9},{9,10},{10,1... | collective-permute-start | bytes 786440 | tf_op jit(solution)/shard_map/while/body/eval_jaxpr/ppermute | solution.py:11
  279.3 11.6 %collective-permute-start = (f32[1,4,128,128]{3,2,1,0:T(8,128)S(1)}, f32[1,4,128,128]{3,2,1,0:T(8,128)S(1)}, u32[]{:S(2)}, u32[]{:S(2)}) collective-permute-start(f32[1,4,128,128]{3,2,1,0:T(8,128)S(1)} %fusion.21), channel_id=1, source_target_pairs={{0,1},{1,2},{2,3},{3,4},{4,5},{5,6},{6,7},{7,8},{8,9},{9,10},{10,1... | collective-permute-start | bytes 786440 | tf_op jit(solution)/shard_map/while/body/eval_jaxpr/ppermute | solution.py:11
  291.1 11.6 %collective-permute-start = (f32[1,4,128,128]{3,2,1,0:T(8,128)S(1)}, f32[1,4,128,128]{3,2,1,0:T(8,128)S(1)}, u32[]{:S(2)}, u32[]{:S(2)}) collective-permute-start(f32[1,4,128,128]{3,2,1,0:T(8,128)S(1)} %fusion.21), channel_id=1, source_target_pairs={{0,1},{1,2},{2,3},{3,4},{4,5},{5,6},{6,7},{7,8},{8,9},{9,10},{10,1... | collective-permute-start | bytes 786440 | tf_op jit(solution)/shard_map/while/body/eval_jaxpr/ppermute | solution.py:11
  302.8 11.6 %collective-permute-start = (f32[1,4,128,128]{3,2,1,0:T(8,128)S(1)}, f32[1,4,128,128]{3,2,1,0:T(8,128)S(1)}, u32[]{:S(2)}, u32[]{:S(2)}) collective-permute-start(f32[1,4,128,128]{3,2,1,0:T(8,128)S(1)} %fusion.21), channel_id=1, source_target_pairs={{0,1},{1,2},{2,3},{3,4},{4,5},{5,6},{6,7},{7,8},{8,9},{9,10},{10,1... | collective-permute-start | bytes 786440 | tf_op jit(solution)/shard_map/while/body/eval_jaxpr/ppermute | solution.py:11
  314.5 11.6 %collective-permute-start = (f32[1,4,128,128]{3,2,1,0:T(8,128)S(1)}, f32[1,4,128,128]{3,2,1,0:T(8,128)S(1)}, u32[]{:S(2)}, u32[]{:S(2)}) collective-permute-start(f32[1,4,128,128]{3,2,1,0:T(8,128)S(1)} %fusion.21), channel_id=1, source_target_pairs={{0,1},{1,2},{2,3},{3,4},{4,5},{5,6},{6,7},{7,8},{8,9},{9,10},{10,1... | collective-permute-start | bytes 786440 | tf_op jit(solution)/shard_map/while/body/eval_jaxpr/ppermute | solution.py:11
  326.3 11.6 %collective-permute-start = (f32[1,4,128,128]{3,2,1,0:T(8,128)S(1)}, f32[1,4,128,128]{3,2,1,0:T(8,128)S(1)}, u32[]{:S(2)}, u32[]{:S(2)}) collective-permute-start(f32[1,4,128,128]{3,2,1,0:T(8,128)S(1)} %fusion.21), channel_id=1, source_target_pairs={{0,1},{1,2},{2,3},{3,4},{4,5},{5,6},{6,7},{7,8},{8,9},{9,10},{10,1... | collective-permute-start | bytes 786440 | tf_op jit(solution)/shard_map/while/body/eval_jaxpr/ppermute | solution.py:11
  338.0 11.6 %collective-permute-start = (f32[1,4,128,128]{3,2,1,0:T(8,128)S(1)}, f32[1,4,128,128]{3,2,1,0:T(8,128)S(1)}, u32[]{:S(2)}, u32[]{:S(2)}) collective-permute-start(f32[1,4,128,128]{3,2,1,0:T(8,128)S(1)} %fusion.21), channel_id=1, source_target_pairs={{0,1},{1,2},{2,3},{3,4},{4,5},{5,6},{6,7},{7,8},{8,9},{9,10},{10,1... | collective-permute-start | bytes 786440 | tf_op jit(solution)/shard_map/while/body/eval_jaxpr/ppermute | solution.py:11
  349.7 11.6 %collective-permute-start = (f32[1,4,128,128]{3,2,1,0:T(8,128)S(1)}, f32[1,4,128,128]{3,2,1,0:T(8,128)S(1)}, u32[]{:S(2)}, u32[]{:S(2)}) collective-permute-start(f32[1,4,128,128]{3,2,1,0:T(8,128)S(1)} %fusion.21), channel_id=1, source_target_pairs={{0,1},{1,2},{2,3},{3,4},{4,5},{5,6},{6,7},{7,8},{8,9},{9,10},{10,1... | collective-permute-start | bytes 786440 | tf_op jit(solution)/shard_map/while/body/eval_jaxpr/ppermute | solution.py:11
  361.5 11.7 %collective-permute-start = (f32[1,4,128,128]{3,2,1,0:T(8,128)S(1)}, f32[1,4,128,128]{3,2,1,0:T(8,128)S(1)}, u32[]{:S(2)}, u32[]{:S(2)}) collective-permute-start(f32[1,4,128,128]{3,2,1,0:T(8,128)S(1)} %fusion.21), channel_id=1, source_target_pairs={{0,1},{1,2},{2,3},{3,4},{4,5},{5,6},{6,7},{7,8},{8,9},{9,10},{10,1... | collective-permute-start | bytes 786440 | tf_op jit(solution)/shard_map/while/body/eval_jaxpr/ppermute | solution.py:11
  387.1 59.1 %copy-start.2 = (f32[512]{0:T(512)S(1)}, f32[512]{0:T(512)}, u32[]{:S(2)}) copy-start(f32[512]{0:T(512)} %param.12) | copy-start | bytes 6148
